TPU v7x, 256 devices: a whole 4x4x8 slice. The times are simulated.
256 devices in a mesh: branch: 8 (over z), mp: 8 (over y_lo, x), dp: 4 (over y_hi, core).
Axes of the slice: x: 4, y: 4 (y_hi: 2, y_lo: 2; y = y_hi * 2 + y_lo), z: 8, core: 2. Of those that a mesh axis runs over, the one named last changes fastest.
Arguments:
- context: bfloat16 [4096, 4096], P(('branch', 'dp'), 'mp'), may hold values from -6 to 6
- residual: bfloat16 [4096, 4096], P(('branch', 'dp')), may hold values from -12 to 12
- attn_weight: bfloat16 [8, 4096, 4096], P('branch', 'mp', 'dp'), may hold values from -0.25 to 0.25
- norm_gain: bfloat16 [4096], replicated, may hold values from 0.099609375 to 1.8984375
- gate_weight: bfloat16 [8, 4096, 5504], P('branch', None, ('mp', 'dp')), may hold values from -0.09375 to 0.09375
- up_weight: bfloat16 [8, 4096, 5504], P('branch', None, ('mp', 'dp')), may hold values from -0.09375 to 0.09375
- down_weight: bfloat16 [8, 5504, 4096], P('branch', ('mp', 'dp')), may hold values from -0.078125 to 0.078125
- cotangent: bfloat16 [4096, 4096], P(('branch', 'dp')), may hold values from -0.796875 to 0.796875
- expert_ids: int32 [4096, 2], P(('branch', 'dp')), may hold values from 0 to 7, as said below
- gate_fixed: int32 [4096, 2], P(('branch', 'dp')), may hold values from 1 to 32767, as said below
Outputs:
- grad_gate: bfloat16 [8, 4096, 5504], P('branch', None, ('mp', 'dp'))
- grad_up: bfloat16 [8, 4096, 5504], P('branch', None, ('mp', 'dp'))
- grad_down: bfloat16 [8, 5504, 4096], P('branch', ('mp', 'dp'))
Inputs may be any that keep to these rules, and one draw needn't show every extreme that they name: `expert_ids`: the two entries of a row differ; in every aligned block of 128 rows some expert is named by more than 40 choices. `gate_fixed`: the two entries of a row sum to 32768.
All inputs are finite; a program needn't handle non-finite values.
Results may differ from a plain program's by a relative error of at most 0.025.
Values may be sent and summed in bfloat16 or wider, within the bound.
A program may use at most 128 MiB of HBM per device.

v0:
```python
import functools
import jax
import jax.numpy as jnp
from jax import lax
from jax.sharding import PartitionSpec as P


def slot_positions(id_block, capacity, experts):
    rows = id_block.shape[0]
    picks = jnp.concatenate([id_block[:, 0], id_block[:, 1]], axis=0)
    onehot = (picks[:, None] == jnp.arange(experts, dtype=jnp.int32)[None, :]).astype(jnp.int32)
    position = jnp.sum((jnp.cumsum(onehot, axis=0) - 1) * onehot, axis=1)
    position = jnp.where(position < capacity, position, -1)
    return jnp.stack([position[:rows], position[rows:]], axis=1)


def expert_pass(weight_set, totals, block_rows, first_row):
    w_gate, w_up, w_down = weight_set
    tokens_in, cotan_rows = block_rows
    pre_gate = jnp.dot(tokens_in, w_gate, preferred_element_type=jnp.float32)
    pre_up = jnp.dot(tokens_in, w_up, preferred_element_type=jnp.float32)
    sigmoid_gate = jax.nn.sigmoid(pre_gate)
    active = pre_gate * sigmoid_gate
    hidden = (active * pre_up).astype(jnp.bfloat16)
    back_grad = lax.dot_general(
        cotan_rows, w_down, (((1,), (1,)), ((), ())), preferred_element_type=jnp.float32
    )
    d_gate = (back_grad * pre_up * sigmoid_gate * (1.0 + pre_gate * (1.0 - sigmoid_gate))).astype(
        jnp.bfloat16
    )
    d_up = (back_grad * active).astype(jnp.bfloat16)
    contract = (((0,), (0,)), ((), ()))
    sum_gate = lax.dot_general(tokens_in, d_gate, contract, preferred_element_type=jnp.float32)
    sum_up = lax.dot_general(tokens_in, d_up, contract, preferred_element_type=jnp.float32)
    sum_down = lax.dot_general(hidden, cotan_rows, contract, preferred_element_type=jnp.float32)
    return (sum_gate, sum_up, sum_down)


def per_device(
    context,
    residual,
    attn_weight,
    norm_gain,
    gate_weight,
    up_weight,
    down_weight,
    cotangent,
    expert_ids,
    gate_fixed,
):
    branches = lax.axis_size("branch")
    summed = lax.psum(attn_weight[0].astype(jnp.float32).astype(jnp.bfloat16), "branch").astype(
        jnp.float32
    )
    merged = (summed / branches).astype(jnp.bfloat16)
    partial_out = jnp.dot(
        context,
        lax.all_gather(merged, "dp", axis=1, tiled=True),
        preferred_element_type=jnp.float32,
    ).astype(jnp.bfloat16)
    attention = lax.psum(partial_out.astype(jnp.float32).astype(jnp.bfloat16), "mp").astype(
        jnp.float32
    )
    mixed_in = residual.astype(jnp.float32) + attention
    inv_rms = lax.rsqrt(jnp.mean(mixed_in * mixed_in, axis=1, keepdims=True) + 1e-05)
    normed = (mixed_in * inv_rms * norm_gain.astype(jnp.float32)[None, :]).astype(jnp.bfloat16)
    model_width = residual.shape[1]
    group_tokens = residual.shape[0]
    experts = branches * gate_weight.shape[0]
    capacity = 5 * group_tokens // (2 * experts)
    slots = slot_positions(expert_ids, capacity, experts)
    slot_share = capacity // lax.axis_size("mp")
    offset = lax.axis_index("mp") * slot_share
    local_slot = slots - offset
    in_share = (slots >= 0) & (local_slot >= 0) & (local_slot < slot_share)
    slot_code = jnp.where(in_share, expert_ids * slot_share + local_slot, -1)
    target = jnp.arange(experts * slot_share, dtype=jnp.int32)
    matches = slot_code[None, :, :] == target[:, None, None]
    selector = jnp.any(matches, axis=2).astype(jnp.bfloat16)
    row_gate = jnp.sum(
        jnp.where(matches, gate_fixed[None, :, :].astype(jnp.float32) / 32768.0, 0.0), axis=(1, 2)
    )
    send_in = jnp.dot(selector, normed, preferred_element_type=jnp.float32).astype(jnp.bfloat16)
    send_in = send_in.reshape(experts, slot_share, model_width)
    cot_rows = jnp.dot(selector, cotangent, preferred_element_type=jnp.float32)
    send_cot = (
        (cot_rows * row_gate[:, None])
        .astype(jnp.bfloat16)
        .reshape(experts, slot_share, model_width)
    )
    hidden_width = gate_weight.shape[2]
    start_totals = (
        jnp.zeros((model_width, hidden_width), jnp.float32),
        jnp.zeros((model_width, hidden_width), jnp.float32),
        jnp.zeros((hidden_width, model_width), jnp.float32),
    )
    accumulate = functools.partial(expert_pass, (gate_weight[0], up_weight[0], down_weight[0]))
    routed_in, routed_cot = (
        lax.all_to_all(send_in, "branch", split_axis=0, concat_axis=1, tiled=True),
        lax.all_to_all(send_cot, "branch", split_axis=0, concat_axis=1, tiled=True),
    )
    totals = accumulate(
        start_totals,
        (
            lax.all_gather(routed_in[0], ("mp", "dp"), axis=0, tiled=True),
            lax.all_gather(routed_cot[0], ("mp", "dp"), axis=0, tiled=True),
        ),
        jnp.int32(0),
    )
    grad_gate = totals[0].astype(jnp.bfloat16)[None]
    grad_up = totals[1].astype(jnp.bfloat16)[None]
    grad_down = totals[2].astype(jnp.bfloat16)[None]
    return (grad_gate, grad_up, grad_down)


def solution(mesh):
    return jax.shard_map(
        per_device,
        mesh=mesh,
        in_specs=(
            P(("branch", "dp"), "mp"),
            P(("branch", "dp"), None),
            P("branch", "mp", "dp"),
            P(),
            P("branch", None, ("mp", "dp")),
            P("branch", None, ("mp", "dp")),
            P("branch", ("mp", "dp"), None),
            P(("branch", "dp"), None),
            P(("branch", "dp"), None),
            P(("branch", "dp"), None),
        ),
        out_specs=(
            P("branch", None, ("mp", "dp")),
            P("branch", None, ("mp", "dp")),
            P("branch", ("mp", "dp"), None),
        ),
        check_vma=False,
    )
```

profile of v0, /device:TPU:1, one launch (start us, length us, event | category | flops | bytes accessed | tf_op | source)
XLA Modules:
  0.0 354.2 jit_solution(13398183778796547387)
XLA Ops:
  8.1 0.7 all-reduce.3.cloned.1.call-update
  8.7 0.0 all-gather.4.cloned.1.call-start
  8.8 77.8 %all-reduce.3.cloned.1.call-done = bf16[512,1024]{1,0:T(8,128)(2,1)} async-done(((bf16[512,1024]{1,0:T(8,128)(2,1)}), bf16[512,1024]{1,0:T(8,128)(2,1)}) %all-reduce.3.cloned.1.call-update) | async-done | bytes 1048592 | tf_op jit(solution)/shard_map/psum | solution.py:52
  86.6 2.4 multiply_convert_fusion.1
  89.0 0.0 all-reduce.5.cloned.1.call-start
  89.1 0.6 reduce-window.6
  89.7 0.2 slice_reduce_fusion
  90.0 0.1 fusion.18
  90.1 43.3 %all-gather.4.cloned.1.call-done = bf16[512,4096]{1,0:T(8,128)(2,1)} async-done(((bf16[512,1024]{1,0:T(8,128)(2,1)}), bf16[512,4096]{1,0:T(8,128)(2,1)}) %all-gather.4.cloned.1.call-update) | async-done | bytes 4194320 | tf_op jit(solution)/shard_map/all_gather | solution.py:58
  133.5 4.5 %fusion.3 = bf16[128,4096]{0,1:T(8,128)(2,1)} fusion(bf16[512,4096]{1,0:T(8,128)(2,1)} %all-gather.4.cloned.1.call-done, bf16[128,512]{1,0:T(8,128)(2,1)S(1)} %copy-done.4), kind=kOutput, calls=%fused_computation.7 | convolution fusion | flops 537395200 | bytes 5373952 | tf_op jit(solution)/shard_map/dot_general | solution.py:56
  138.0 0.0 all-gather.8.cloned.1.call-start
  138.0 0.1 select_reduce_fusion
  138.2 0.3 fusion.4
  138.5 0.1 reshape.54
  138.6 24.0 %all_to_all.8 = bf16[8,5,4096]{2,1,0:T(8,128)(2,1)S(1)} all-to-all(bf16[8,5,4096]{2,1,0:T(8,128)(2,1)S(1)} %reshape.54), channel_id=1, replica_groups=mesh['branch'=8,'mp'=8,'dp'=4] {'branch'}, dimensions={0} | all-to-all | bytes 655360 | tf_op jit(solution)/shard_map/all_to_all | solution.py:100
  162.6 0.9 squeeze.28
  163.5 0.0 all-gather.6.cloned.1.call-start
  163.6 0.6 convert_element_type.69
  164.2 0.7 copy.19
  164.9 61.1 %all-reduce.5.cloned.1.call-done = bf16[128,4096]{0,1:T(8,128)(2,1)} async-done(((bf16[128,4096]{0,1:T(8,128)(2,1)}), bf16[128,4096]{0,1:T(8,128)(2,1)}) %all-reduce.5.cloned.1.call-update) | async-done | bytes 1048592 | tf_op jit(solution)/shard_map/psum | solution.py:61
  226.0 1.9 multiply_reduce_fusion
  227.9 1.0 convolution_convert_fusion.4
  228.9 0.1 reshape.53
  229.1 21.5 %all_to_all.9 = bf16[8,5,4096]{2,1,0:T(8,128)(2,1)S(1)} all-to-all(bf16[8,5,4096]{2,1,0:T(8,128)(2,1)S(1)} %reshape.53), channel_id=1, replica_groups=mesh['branch'=8,'mp'=8,'dp'=4] {'branch'}, dimensions={0} | all-to-all | bytes 655360 | tf_op jit(solution)/shard_map/all_to_all | solution.py:99
  250.5 0.9 squeeze.27
  251.5 8.6 %fusion.9 = f32[1280,172]{0,1:T(8,128)} fusion(bf16[1280,4096]{1,0:T(8,128)(2,1)} %all-gather.8.cloned.1.call-done, bf16[1,172,4096]{2,1,0:T(8,128)(2,1)S(1)} %copy-done), kind=kOutput, calls=%fused_computation.19 | convolution fusion | flops 1803550720 | bytes 12775424 | tf_op jit(solution)/shard_map/dot_general | solution.py:25
  260.1 61.2 %all-gather.6.cloned.1.call-done = bf16[1280,4096]{1,0:T(8,128)(2,1)} async-done(((bf16[40,4096]{1,0:T(8,128)(2,1)}), bf16[1280,4096]{1,0:T(8,128)(2,1)}) %all-gather.6.cloned.1.call-update) | async-done | bytes 10485776 | tf_op jit(solution)/shard_map/all_gather | solution.py:105
  321.3 7.8 %fusion.5 = f32[1280,172]{0,1:T(8,128)S(1)} fusion(bf16[1280,4096]{1,0:T(8,128)(2,1)} %all-gather.6.cloned.1.call-done, bf16[1,4096,172]{1,2,0:T(8,128)(2,1)S(1)} %copy-done.9), kind=kOutput, calls=%fused_computation.15 | convolution fusion | flops 1803550720 | bytes 12775424 | tf_op jit(solution)/shard_map/dot_general | solution.py:20
  329.1 7.8 %fusion.7 = f32[1280,172]{0,1:T(8,128)S(1)} fusion(bf16[1280,4096]{1,0:T(8,128)(2,1)} %all-gather.6.cloned.1.call-done, bf16[1,4096,172]{1,2,0:T(8,128)(2,1)S(1)} %copy-done.10), kind=kOutput, calls=%fused_computation.17 | convolution fusion | flops 1803550720 | bytes 12775424 | tf_op jit(solution)/shard_map/dot_general | solution.py:21
  336.9 3.2 fusion.2
  340.2 3.5 fusion
  343.7 3.3 fusion.1
  (55 shorter events, 0.3 us)
Async XLA Ops:
  8.0 243.5 %copy-start = (bf16[1,172,4096]{2,1,0:T(8,128)(2,1)S(1)}, bf16[1,172,4096]{2,1,0:T(8,128)(2,1)}, u32[]{:S(2)}) copy-start(bf16[1,172,4096]{2,1,0:T(8,128)(2,1)} %param.16) | copy-start | bytes 4227076
  8.0 78.6 %all-reduce.3.cloned.1.call-start = ((), (), s32[]{:S(2)}) async-start(), calls=%async_computation.2 | async-start | bytes 2097152 | tf_op jit(solution)/shard_map/psum | solution.py:52
  8.1 81.0 %copy-start.7 = (s32[128,2]{0,1:T(2,128)S(1)}, s32[128,2]{0,1:T(2,128)}, u32[]{:S(2)}) copy-start(s32[128,2]{0,1:T(2,128)} %param.18) | copy-start | bytes 3076
  8.1 82.0 %copy-start.8 = (s32[128,2]{0,1:T(2,128)S(1)}, s32[128,2]{0,1:T(2,128)}, u32[]{:S(2)}) copy-start(s32[128,2]{0,1:T(2,128)} %param.19) | copy-start | bytes 3076
  8.1 125.4 %copy-start.4 = (bf16[128,512]{1,0:T(8,128)(2,1)S(1)}, bf16[128,512]{1,0:T(8,128)(2,1)}, u32[]{:S(2)}) copy-start(bf16[128,512]{1,0:T(8,128)(2,1)} %param.10) | copy-start | bytes 393220
  8.7 124.7 %all-gather.4.cloned.1.call-start = ((), (), s32[]{:S(2)}) async-start(), calls=%async_computation.3 | async-start | bytes 5242880 | tf_op jit(solution)/shard_map/all_gather | solution.py:58
  89.0 137.0 %all-reduce.5.cloned.1.call-start = ((), (), s32[]{:S(2)}) async-start(), calls=%async_computation.4 | async-start | bytes 2097152 | tf_op jit(solution)/shard_map/psum | solution.py:61
  90.1 48.0 %copy-start.2 = (bf16[128,4096]{1,0:T(8,128)(2,1)S(1)}, bf16[128,4096]{1,0:T(8,128)(2,1)}, u32[]{:S(2)}) copy-start(bf16[128,4096]{1,0:T(8,128)(2,1)} %param.17) | copy-start | bytes 3145732
  138.0 113.5 %all-gather.8.cloned.1.call-start = ((), (), s32[]{:S(2)}) async-start(), calls=%async_computation.6 | async-start | bytes 10813440 | tf_op jit(solution)/shard_map/all_gather | solution.py:106
  138.2 25.4 %copy-start.6 = (bf16[4096]{0:T(1024)(128)(2,1)S(1)}, bf16[4096]{0:T(1024)(128)(2,1)}, u32[]{:S(2)}) copy-start(bf16[4096]{0:T(1024)(128)(2,1)} %param.13) | copy-start | bytes 24580
  138.5 25.7 %copy-start.3 = (bf16[128,4096]{1,0:T(8,128)(2,1)S(1)}, bf16[128,4096]{1,0:T(8,128)(2,1)}, u32[]{:S(2)}) copy-start(bf16[128,4096]{1,0:T(8,128)(2,1)} %param.11) | copy-start | bytes 3145732
  163.5 157.8 %all-gather.6.cloned.1.call-start = ((), (), s32[]{:S(2)}) async-start(), calls=%async_computation.5 | async-start | bytes 10813440 | tf_op jit(solution)/shard_map/all_gather | solution.py:105
  164.9 63.0 %copy-start.5 = (f32[4096]{0:T(1024)S(1)}, f32[4096]{0:T(1024)}, u32[]{:S(2)}) copy-start(f32[4096]{0:T(1024)} %convert_element_type.69) | copy-start | bytes 49156
  226.0 1.9 copy-start.1
  251.4 69.9 %copy-start.9 = (bf16[1,4096,172]{1,2,0:T(8,128)(2,1)S(1)}, bf16[1,4096,172]{1,2,0:T(8,128)(2,1)}, u32[]{:S(2)}) copy-start(bf16[1,4096,172]{1,2,0:T(8,128)(2,1)} %param.14) | copy-start | bytes 4227076
  321.3 7.8 %copy-start.10 = (bf16[1,4096,172]{1,2,0:T(8,128)(2,1)S(1)}, bf16[1,4096,172]{1,2,0:T(8,128)(2,1)}, u32[]{:S(2)}) copy-start(bf16[1,4096,172]{1,2,0:T(8,128)(2,1)} %param.15) | copy-start | bytes 4227076
  321.3 15.6 %slice-start = ((s8[10485760]{0:T(1024)(128)(4,1)}), s8[4194304]{0:T(1024)(128)(4,1)S(1)}, s32[]{:S(2)}) async-start(s8[10485760]{0:T(1024)(128)(4,1)} %bitcast.46), calls=%async_computation.7 | async-start | bytes 8388608
  321.3 15.6 %slice-start.1 = ((s8[10485760]{0:T(1024)(128)(4,1)}), s8[4194304]{0:T(1024)(128)(4,1)S(1)}, s32[]{:S(2)}) async-start(s8[10485760]{0:T(1024)(128)(4,1)} %bitcast.46), calls=%async_computation.8 | async-start | bytes 8388608
  329.1 7.8 %slice-start.2 = ((s8[10485760]{0:T(1024)(128)(4,1)}), s8[2097152]{0:T(1024)(128)(4,1)S(1)}, s32[]{:S(2)}) async-start(s8[10485760]{0:T(1024)(128)(4,1)} %bitcast.46), calls=%async_computation.9 | async-start | bytes 4194304
  329.1 11.1 %slice-start.3 = ((s8[10485760]{0:T(1024)(128)(4,1)}), s8[4194304]{0:T(1024)(128)(4,1)S(1)}, s32[]{:S(2)}) async-start(s8[10485760]{0:T(1024)(128)(4,1)} %bitcast.48), calls=%async_computation.10 | async-start | bytes 8388608
  329.1 11.1 %slice-start.4 = ((s8[10485760]{0:T(1024)(128)(4,1)}), s8[4194304]{0:T(1024)(128)(4,1)S(1)}, s32[]{:S(2)}) async-start(s8[10485760]{0:T(1024)(128)(4,1)} %bitcast.48), calls=%async_computation.11 | async-start | bytes 8388608
  336.9 3.3 slice-start.5
  336.9 3.3 copy-start.11
Sparse Core Ops, SparseCore 0:
  11.2 75.3 all-reduce.2
  89.1 44.2 all-gather.3
  138.1 87.8 all-reduce.4
Sparse Core Ops, SparseCore 1:
  163.6 76.4 all-gather.7
  251.5 69.8 all-gather.5
where the time goes:
time: 354 us
  waiting for transfers between devices  244 us (69%)
  blocking collectives  45.5 us (13%)
  matrix products  40 us (11%)
  between operations  15.5 us (4%)
  other arithmetic  5.78 us (2%)
    psum x1, waiting for transfers between devices, per_device(): lax.psum(attn_weight[0].astype(jnp.float32).astype(jnp.bfloat16), 'branch')  77.8 us
    all_gather x1, waiting for transfers between devices, per_device(): lax.all_gather(routed_in[0], ('mp', 'dp'), axis=0, tiled=True)  61.2 us
    psum x1, waiting for transfers between devices, per_device(): lax.psum(partial_out.astype(jnp.float32).astype(jnp.bfloat16), 'mp')  61.1 us
    all_gather x1, waiting for transfers between devices, per_device(): lax.all_gather(merged, 'dp', axis=1, tiled=True)  43.3 us
    all_to_all x1, blocking collectives, per_device(): lax.all_to_all(send_cot, 'branch', split_axis=0, concat_axis=1, tiled=True)  24 us
    all_to_all x1, blocking collectives, per_device(): lax.all_to_all(send_in, 'branch', split_axis=0, concat_axis=1, tiled=True)  21.5 us
    dot_general x1, matrix products, expert_pass(): lax.dot_general(cotan_rows, w_down, (((1,), (1,)), ((), ())), preferred_e...  8.63 us
    dot_general x1, matrix products, expert_pass(): pre_gate = jnp.dot(tokens_in, w_gate, preferred_element_type=jnp.float32)  7.76 us
  transfers between devices with their start and end apart: 5, of which 4 were waited for; matrix products, arithmetic and copies ran while one was open for 5% of the time, Pallas kernels for 0%

commit v1 on v0

--- a/solution.py
+++ b/solution.py
@@ -102,7 +102,12 @@
     totals = accumulate(
         start_totals,
         (
-            lax.all_gather(routed_in[0], ("mp", "dp"), axis=0, tiled=True),
+            jnp.concatenate(
+                lax.all_to_all(
+                    jnp.stack([routed_in[0]] * lax.axis_size(("mp", "dp"))), ("mp", "dp"), 0, 0
+                ),
+                axis=0,
+            ),
             lax.all_gather(routed_cot[0], ("mp", "dp"), axis=0, tiled=True),
         ),
         jnp.int32(0),

time: 354 us -> 413 us (1.17)
  blocking collectives: 45.5 us -> 173 us
  waiting for transfers between devices: 244 us -> 183 us
  matrix products: 40 us -> 32.6 us
    all_to_all x0 -> x1, blocking collectives: none -> 128 us  [per_device(): lax.all_to_all(jnp.stack([routed_in[0]] * lax.axis_size(('mp', 'dp'))), (...]
    all_gather x1 -> x0, waiting for transfers between devices: 61.2 us -> none  [per_device(): lax.all_gather(routed_in[0], ('mp', 'dp'), axis=0, tiled=True)]
  transfers between devices with their start and end apart: 5 -> 4, of which waited for: 4 -> 3; matrix products, arithmetic and copies ran while one was open for 5% -> 4% of each run, Pallas kernels for 0% -> 0%
where the time goes in v1:
time: 413 us
  waiting for transfers between devices  183 us (44%)
  blocking collectives  173 us (42%)
  matrix products  32.6 us (8%)
  between operations  15.5 us (4%)
  other arithmetic  5.17 us (1%)
    all_to_all x1, blocking collectives, per_device(): lax.all_to_all(jnp.stack([routed_in[0]] * lax.axis_size(('mp', 'dp'))), (...  128 us
    psum x1, waiting for transfers between devices, per_device(): lax.psum(attn_weight[0].astype(jnp.float32).astype(jnp.bfloat16), 'branch')  77.8 us
    psum x1, waiting for transfers between devices, per_device(): lax.psum(partial_out.astype(jnp.float32).astype(jnp.bfloat16), 'mp')  60.9 us
    all_gather x1, waiting for transfers between devices, per_device(): lax.all_gather(merged, 'dp', axis=1, tiled=True)  43.3 us
    all_to_all x1, blocking collectives, per_device(): lax.all_to_all(send_cot, 'branch', split_axis=0, concat_axis=1, tiled=True)  24 us
    all_to_all x1, blocking collectives, per_device(): lax.all_to_all(send_in, 'branch', split_axis=0, concat_axis=1, tiled=True)  21 us
  transfers between devices with their start and end apart: 4, of which 3 were waited for; matrix products, arithmetic and copies ran while one was open for 4% of the time, Pallas kernels for 0%

profile of v1, /device:TPU:1, one launch (start us, length us, event | category | flops | bytes accessed | tf_op | source)
XLA Modules:
  0.0 412.9 jit_solution(11387495929308807610)
XLA Ops:
  8.0 0.0 all-reduce.3.cloned.1.call-start
  8.1 0.7 all-reduce.3.cloned.1.call-update
  8.7 0.0 all-gather.3.cloned.1.call-start
  8.8 77.8 %all-reduce.3.cloned.1.call-done = bf16[512,1024]{1,0:T(8,128)(2,1)} async-done(((bf16[512,1024]{1,0:T(8,128)(2,1)}), bf16[512,1024]{1,0:T(8,128)(2,1)}) %all-reduce.3.cloned.1.call-update) | async-done | bytes 1048592 | tf_op jit(solution)/shard_map/psum | solution.py:52
  86.6 2.4 multiply_convert_fusion.1
  89.0 0.0 all-reduce.5.cloned.1.call-start
  89.1 0.6 reduce-window.6
  89.7 0.2 slice_reduce_fusion
  90.0 0.1 fusion.18
  90.1 43.3 %all-gather.3.cloned.1.call-done = bf16[512,4096]{1,0:T(8,128)(2,1)} async-done(((bf16[512,1024]{1,0:T(8,128)(2,1)}), bf16[512,4096]{1,0:T(8,128)(2,1)}) %all-gather.3.cloned.1.call-update) | async-done | bytes 4194320 | tf_op jit(solution)/shard_map/all_gather | solution.py:58
  133.5 4.5 %fusion.3 = bf16[128,4096]{0,1:T(8,128)(2,1)} fusion(bf16[512,4096]{1,0:T(8,128)(2,1)} %all-gather.3.cloned.1.call-done, bf16[128,512]{1,0:T(8,128)(2,1)S(1)} %copy-done.6), kind=kOutput, calls=%fused_computation.7 | convolution fusion | flops 537395200 | bytes 5373952 | tf_op jit(solution)/shard_map/dot_general | solution.py:56
  138.0 0.0 all-gather.5.cloned.1.call-start
  138.0 0.1 select_reduce_fusion
  138.2 0.3 fusion.4
  138.5 0.1 reshape.59
  138.6 24.0 %all_to_all.26 = bf16[8,5,4096]{2,1,0:T(8,128)(2,1)S(1)} all-to-all(bf16[8,5,4096]{2,1,0:T(8,128)(2,1)S(1)} %reshape.59), channel_id=1, replica_groups=mesh['branch'=8,'mp'=8,'dp'=4] {'branch'}, dimensions={0} | all-to-all | bytes 655360 | tf_op jit(solution)/shard_map/all_to_all | solution.py:100
  162.6 0.9 squeeze.24
  163.5 0.7 copy.19
  164.2 60.9 %all-reduce.5.cloned.1.call-done = bf16[128,4096]{0,1:T(8,128)(2,1)} async-done(((bf16[128,4096]{0,1:T(8,128)(2,1)}), bf16[128,4096]{0,1:T(8,128)(2,1)}) %all-reduce.5.cloned.1.call-update) | async-done | bytes 1048592 | tf_op jit(solution)/shard_map/psum | solution.py:61
  225.1 1.9 multiply_reduce_fusion
  227.0 1.0 convolution_convert_fusion.4
  228.0 0.1 reshape.57
  228.2 21.0 %all_to_all.27 = bf16[8,5,4096]{2,1,0:T(8,128)(2,1)S(1)} all-to-all(bf16[8,5,4096]{2,1,0:T(8,128)(2,1)S(1)} %reshape.57), channel_id=1, replica_groups=mesh['branch'=8,'mp'=8,'dp'=4] {'branch'}, dimensions={0} | all-to-all | bytes 655360 | tf_op jit(solution)/shard_map/all_to_all | solution.py:99
  249.1 0.1 all_to_all.9
  249.3 1.3 stack.15
  250.6 128.2 %all_to_all.28 = bf16[32,40,4096]{2,1,0:T(8,128)(2,1)S(1)} all-to-all(bf16[32,40,4096]{2,1,0:T(8,128)(2,1)S(1)} %stack.15), channel_id=1, replica_groups=mesh['branch'=8,'mp'=8,'dp'=4] {'mp','dp'}, dimensions={0} | all-to-all | bytes 20971520 | tf_op jit(solution)/shard_map/all_to_all | solution.py:106
  378.8 4.5 %fusion.5 = f32[1280,172]{0,1:T(8,128)} fusion(bf16[1280,4096]{1,0:T(8,128)(2,1)S(1)} %bitcast.46, bf16[1,4096,172]{1,2,0:T(8,128)(2,1)S(1)} %copy-done), kind=kOutput, calls=%fused_computation.15 | convolution fusion | flops 1803550720 | bytes 12775424 | tf_op jit(solution)/shard_map/dot_general | solution.py:20
  383.3 4.5 %fusion.7 = f32[1280,172]{0,1:T(8,128)} fusion(bf16[1280,4096]{1,0:T(8,128)(2,1)S(1)} %bitcast.47, bf16[1,4096,172]{1,2,0:T(8,128)(2,1)S(1)} %copy-done.10), kind=kOutput, calls=%fused_computation.17 | convolution fusion | flops 1803550720 | bytes 12775424 | tf_op jit(solution)/shard_map/dot_general | solution.py:21
  387.9 7.8 %fusion.9 = f32[1280,172]{0,1:T(8,128)S(1)} fusion(bf16[1280,4096]{1,0:T(8,128)(2,1)} %all-gather.5.cloned.1.call-done, bf16[1,172,4096]{2,1,0:T(8,128)(2,1)S(1)} %copy-done.11), kind=kOutput, calls=%fused_computation.19 | convolution fusion | flops 1803550720 | bytes 12775424 | tf_op jit(solution)/shard_map/dot_general | solution.py:25
  395.7 3.3 fusion.1
  399.0 3.5 fusion
  402.5 3.2 fusion.2
  (51 shorter events, 0.2 us)
Async XLA Ops:
  8.0 370.8 %copy-start = (bf16[1,4096,172]{1,2,0:T(8,128)(2,1)S(1)}, bf16[1,4096,172]{1,2,0:T(8,128)(2,1)}, u32[]{:S(2)}) copy-start(bf16[1,4096,172]{1,2,0:T(8,128)(2,1)} %param.14) | copy-start | bytes 4227076
  8.0 78.6 %all-reduce.3.cloned.1.call-start = ((), (), s32[]{:S(2)}) async-start(), calls=%async_computation.3 | async-start | bytes 2097152 | tf_op jit(solution)/shard_map/psum | solution.py:52
  8.1 81.0 %copy-start.8 = (s32[128,2]{0,1:T(2,128)S(1)}, s32[128,2]{0,1:T(2,128)}, u32[]{:S(2)}) copy-start(s32[128,2]{0,1:T(2,128)} %param.18) | copy-start | bytes 3076
  8.1 82.0 %copy-start.9 = (s32[128,2]{0,1:T(2,128)S(1)}, s32[128,2]{0,1:T(2,128)}, u32[]{:S(2)}) copy-start(s32[128,2]{0,1:T(2,128)} %param.19) | copy-start | bytes 3076
  8.1 125.4 %copy-start.6 = (bf16[128,512]{1,0:T(8,128)(2,1)S(1)}, bf16[128,512]{1,0:T(8,128)(2,1)}, u32[]{:S(2)}) copy-start(bf16[128,512]{1,0:T(8,128)(2,1)} %param.10) | copy-start | bytes 393220
  8.7 124.7 %all-gather.3.cloned.1.call-start = ((), (), s32[]{:S(2)}) async-start(), calls=%async_computation.4 | async-start | bytes 5242880 | tf_op jit(solution)/shard_map/all_gather | solution.py:58
  89.0 136.1 %all-reduce.5.cloned.1.call-start = ((), (), s32[]{:S(2)}) async-start(), calls=%async_computation.5 | async-start | bytes 2097152 | tf_op jit(solution)/shard_map/psum | solution.py:61
  90.1 48.0 %copy-start.4 = (bf16[128,4096]{1,0:T(8,128)(2,1)S(1)}, bf16[128,4096]{1,0:T(8,128)(2,1)}, u32[]{:S(2)}) copy-start(bf16[128,4096]{1,0:T(8,128)(2,1)} %param.17) | copy-start | bytes 3145732
  138.0 249.9 %all-gather.5.cloned.1.call-start = ((), (), s32[]{:S(2)}) async-start(), calls=%async_computation.6 | async-start | bytes 10813440 | tf_op jit(solution)/shard_map/all_gather | solution.py:111
  138.4 25.1 %copy-start.5 = (bf16[128,4096]{1,0:T(8,128)(2,1)S(1)}, bf16[128,4096]{1,0:T(8,128)(2,1)}, u32[]{:S(2)}) copy-start(bf16[128,4096]{1,0:T(8,128)(2,1)} %param.11) | copy-start | bytes 3145732
  138.6 25.6 %copy-start.7 = (bf16[4096]{0:T(1024)(128)(2,1)S(1)}, bf16[4096]{0:T(1024)(128)(2,1)}, u32[]{:S(2)}) copy-start(bf16[4096]{0:T(1024)(128)(2,1)} %param.13) | copy-start | bytes 24580
  225.1 1.9 copy-start.3
  378.8 4.5 %copy-start.1 = (bf16[32,40,4096]{2,1,0:T(8,128)(2,1)}, bf16[32,40,4096]{2,1,0:T(8,128)(2,1)S(1)}, u32[]{:S(2)}) copy-start(bf16[32,40,4096]{2,1,0:T(8,128)(2,1)S(1)} %all_to_all.28) | copy-start | bytes 31457284
  378.8 4.5 %copy-start.10 = (bf16[1,4096,172]{1,2,0:T(8,128)(2,1)S(1)}, bf16[1,4096,172]{1,2,0:T(8,128)(2,1)}, u32[]{:S(2)}) copy-start(bf16[1,4096,172]{1,2,0:T(8,128)(2,1)} %param.15) | copy-start | bytes 4227076
  383.3 4.5 %copy-start.11 = (bf16[1,172,4096]{2,1,0:T(8,128)(2,1)S(1)}, bf16[1,172,4096]{2,1,0:T(8,128)(2,1)}, u32[]{:S(2)}) copy-start(bf16[1,172,4096]{2,1,0:T(8,128)(2,1)} %param.16) | copy-start | bytes 4227076
  387.8 7.8 %copy-start.2 = (bf16[32,40,4096]{2,1,0:T(8,128)(2,1)S(1)}, bf16[32,40,4096]{2,1,0:T(8,128)(2,1)}, u32[]{:S(2)}) copy-start(bf16[32,40,4096]{2,1,0:T(8,128)(2,1)} %copy-done.1) | copy-start | bytes 31457284
  387.9 7.8 %copy-start.12 = (f32[1280,172]{0,1:T(8,128)S(1)}, f32[1280,172]{0,1:T(8,128)}, u32[]{:S(2)}) copy-start(f32[1280,172]{0,1:T(8,128)} %fusion.5) | copy-start | bytes 2641924
  395.6 3.3 copy-start.13
  395.6 6.9 %slice-start = ((s8[10485760]{0:T(1024)(128)(4,1)}), s8[4194304]{0:T(1024)(128)(4,1)S(1)}, s32[]{:S(2)}) async-start(s8[10485760]{0:T(1024)(128)(4,1)} %bitcast.51), calls=%async_computation.7 | async-start | bytes 8388608
  395.7 6.8 %slice-start.1 = ((s8[10485760]{0:T(1024)(128)(4,1)}), s8[4194304]{0:T(1024)(128)(4,1)S(1)}, s32[]{:S(2)}) async-start(s8[10485760]{0:T(1024)(128)(4,1)} %bitcast.51), calls=%async_computation.8 | async-start | bytes 8388608
  399.0 3.5 slice-start.2
Sparse Core Ops, SparseCore 0:
  11.2 75.3 all-reduce.2
  89.1 44.2 all-gather.2
  138.1 86.9 all-reduce.4
Sparse Core Ops, SparseCore 1:
  163.6 76.5 all-gather.4
